TPU v7x, 512 devices: a whole 4x4x16 slice. The times are simulated.
512 devices in a mesh: row: 8 (over y, z_hi), col: 16 (over z_lo, core), depth: 4 (over x).
Axes of the slice: x: 4, y: 4, z: 16 (z_hi: 2, z_lo: 8; z = z_hi * 8 + z_lo), core: 2. Of those that a mesh axis runs over, the one named last changes fastest.
Arguments:
- a_tiles: bfloat16 [8, 16, 4, 4, 128, 128], P('row', 'col', 'depth'), may hold values from -0.625 to 0.625
- pair_lists: int32 [8, 16, 4, 16, 2, 4, 12], P('row', 'col', 'depth'), may hold values from 0 to 31, as said below
Outputs:
- product_blocks: float32 [8, 16, 12, 128, 128], P('row', 'col', 'depth')
Inputs may be any that keep to these rules, and one draw needn't show every extreme that they name: pair_lists[..., 0, m, o] is a left slot below 4, or 4 for an empty pair slot; the live pairs of a product block come first; pair_lists[..., 1, m, o] is a slot of the right panel.
All inputs are finite; a program needn't handle non-finite values.
Results may differ from a plain program's by a relative error of at most 0.0003.
Values may be sent and summed in bfloat16 or wider, within the bound.
A program may use at most 64 MiB of HBM per device.

v0:
```python
import jax
import jax.numpy as jnp
from jax import lax
from jax.sharding import PartitionSpec as P


def from_behind(block, axis, distance):
    devices = range(lax.axis_size(axis))
    route = [((i - distance) % len(devices), i) for i in devices]
    return lax.ppermute(block, axis, route)


def body(a_tiles, pair_lists):
    slot_count = a_tiles.shape[3]
    block_width = a_tiles.shape[4]
    own_tiles = a_tiles.reshape(slot_count, block_width, block_width)
    pair_table = pair_lists.reshape(pair_lists.shape[3:])
    shift_count = pair_table.shape[0]
    right_panel = lax.all_gather(own_tiles, "row", axis=0, tiled=True)
    zero_block = jnp.zeros((1, block_width, block_width), jnp.bfloat16)

    def contract(left_set, left_index, right_index):
        chosen = jnp.take(left_set, left_index, axis=0)
        partner = jnp.take(right_panel, right_index, axis=0)
        return jnp.einsum("moik,mojk->oij", chosen, partner, preferred_element_type=jnp.float32)

    def advance(step_index, carried):
        panel_tile, running = carried
        shifted = from_behind(panel_tile, "col", 1)
        padded = jnp.concatenate([shifted, zero_block], axis=0)
        return (
            shifted,
            running + contract(padded, pair_table[step_index, 0], pair_table[step_index, 1]),
        )

    opening = contract(
        jnp.concatenate([own_tiles, zero_block], axis=0), pair_table[0, 0], pair_table[0, 1]
    )
    carried = lax.fori_loop(1, shift_count, advance, (own_tiles, opening))
    running = carried[1]
    reduced = lax.psum_scatter(running, "depth", scatter_dimension=0, tiled=True)
    return reduced.reshape((1, 1) + reduced.shape)


def solution(mesh):
    placed = (
        P("row", "col", "depth", None, None, None),
        P("row", "col", "depth", None, None, None, None),
    )
    return jax.shard_map(
        body,
        mesh=mesh,
        in_specs=placed,
        out_specs=P("row", "col", "depth", None, None),
        check_vma=False,
    )
```

profile of v0, /device:TPU:6, one launch (start us, length us, event | category | flops | bytes accessed | tf_op | source)
XLA Modules:
  0.0 408.5 jit_solution(16223850005393163813)
XLA Ops:
  11.3 94.9 %all-gather.3.cloned.1.call-done = bf16[1,1,1,32,128,128]{5,4,2,1,0,3:T(8,128)(2,1)} async-done(((bf16[1,1,1,4,128,128]{5,4,2,1,0,3:T(8,128)(2,1)}), bf16[1,1,1,32,128,128]{5,4,2,1,0,3:T(8,128)(2,1)}) %all-gather.3.cloned.1.call-update) | async-done | bytes 1048592 | tf_op jit(solution)/shard_map/all_gather | solution.py:19
  106.2 3.2 gather_fusion.3
  112.4 270.5 %while.17 = (s32[]{:T(128)}, bf16[4,128,128]{2,1,0:T(8,128)(2,1)S(1)}, f32[12,128,128]{2,1,0:T(8,128)}, s32[16,2,4,12]{3,2,1,0:T(4,128)S(1)}, bf16[32,128,128]{2...) while((s32[]{:T(128)}, bf16[4,128,128]{2,1,0:T(8,128)(2,1)S(1)}, ...), condition=%wide.region_1.0_spmd, body=%wide.region_0.3_spmd.sunk | while | flops 203098688 | bytes 12102445 | solution.py:39
  115.6 9.7 %collective-permute-done = bf16[4,128,128]{2,1,0:T(8,128)(2,1)S(1)} collective-permute-done((bf16[4,128,128]{2,1,0:T(8,128)(2,1)S(1)}, bf16[4,128,128]{2,1,0:T(8,128)(2,1)S(1)}, u32[]{:S(2)}, u32[]{:S(2)}) %collective-permute-start) | collective-permute-done | bytes 131104 | tf_op jit(solution)/shard_map/while/body/eval_jaxpr/ppermute | solution.py:10
  127.3 3.1 fusion.14
  133.7 9.7 %collective-permute-done = bf16[4,128,128]{2,1,0:T(8,128)(2,1)S(1)} collective-permute-done((bf16[4,128,128]{2,1,0:T(8,128)(2,1)S(1)}, bf16[4,128,128]{2,1,0:T(8,128)(2,1)S(1)}, u32[]{:S(2)}, u32[]{:S(2)}) %collective-permute-start) | collective-permute-done | bytes 131104 | tf_op jit(solution)/shard_map/while/body/eval_jaxpr/ppermute | solution.py:10
  145.3 3.1 fusion.14
  151.7 9.7 %collective-permute-done = bf16[4,128,128]{2,1,0:T(8,128)(2,1)S(1)} collective-permute-done((bf16[4,128,128]{2,1,0:T(8,128)(2,1)S(1)}, bf16[4,128,128]{2,1,0:T(8,128)(2,1)S(1)}, u32[]{:S(2)}, u32[]{:S(2)}) %collective-permute-start) | collective-permute-done | bytes 131104 | tf_op jit(solution)/shard_map/while/body/eval_jaxpr/ppermute | solution.py:10
  163.3 3.1 fusion.14
  169.7 9.7 %collective-permute-done = bf16[4,128,128]{2,1,0:T(8,128)(2,1)S(1)} collective-permute-done((bf16[4,128,128]{2,1,0:T(8,128)(2,1)S(1)}, bf16[4,128,128]{2,1,0:T(8,128)(2,1)S(1)}, u32[]{:S(2)}, u32[]{:S(2)}) %collective-permute-start) | collective-permute-done | bytes 131104 | tf_op jit(solution)/shard_map/while/body/eval_jaxpr/ppermute | solution.py:10
  181.4 3.1 fusion.14
  187.8 9.7 %collective-permute-done = bf16[4,128,128]{2,1,0:T(8,128)(2,1)S(1)} collective-permute-done((bf16[4,128,128]{2,1,0:T(8,128)(2,1)S(1)}, bf16[4,128,128]{2,1,0:T(8,128)(2,1)S(1)}, u32[]{:S(2)}, u32[]{:S(2)}) %collective-permute-start) | collective-permute-done | bytes 131104 | tf_op jit(solution)/shard_map/while/body/eval_jaxpr/ppermute | solution.py:10
  199.4 3.1 fusion.14
  205.8 9.7 %collective-permute-done = bf16[4,128,128]{2,1,0:T(8,128)(2,1)S(1)} collective-permute-done((bf16[4,128,128]{2,1,0:T(8,128)(2,1)S(1)}, bf16[4,128,128]{2,1,0:T(8,128)(2,1)S(1)}, u32[]{:S(2)}, u32[]{:S(2)}) %collective-permute-start) | collective-permute-done | bytes 131104 | tf_op jit(solution)/shard_map/while/body/eval_jaxpr/ppermute | solution.py:10
  217.5 3.1 fusion.14
  223.9 9.7 %collective-permute-done = bf16[4,128,128]{2,1,0:T(8,128)(2,1)S(1)} collective-permute-done((bf16[4,128,128]{2,1,0:T(8,128)(2,1)S(1)}, bf16[4,128,128]{2,1,0:T(8,128)(2,1)S(1)}, u32[]{:S(2)}, u32[]{:S(2)}) %collective-permute-start) | collective-permute-done | bytes 131104 | tf_op jit(solution)/shard_map/while/body/eval_jaxpr/ppermute | solution.py:10
  235.5 3.1 fusion.14
  241.9 9.7 %collective-permute-done = bf16[4,128,128]{2,1,0:T(8,128)(2,1)S(1)} collective-permute-done((bf16[4,128,128]{2,1,0:T(8,128)(2,1)S(1)}, bf16[4,128,128]{2,1,0:T(8,128)(2,1)S(1)}, u32[]{:S(2)}, u32[]{:S(2)}) %collective-permute-start) | collective-permute-done | bytes 131104 | tf_op jit(solution)/shard_map/while/body/eval_jaxpr/ppermute | solution.py:10
  253.5 3.1 fusion.14
  259.9 9.7 %collective-permute-done = bf16[4,128,128]{2,1,0:T(8,128)(2,1)S(1)} collective-permute-done((bf16[4,128,128]{2,1,0:T(8,128)(2,1)S(1)}, bf16[4,128,128]{2,1,0:T(8,128)(2,1)S(1)}, u32[]{:S(2)}, u32[]{:S(2)}) %collective-permute-start) | collective-permute-done | bytes 131104 | tf_op jit(solution)/shard_map/while/body/eval_jaxpr/ppermute | solution.py:10
  271.6 3.1 fusion.14
  278.0 9.7 %collective-permute-done = bf16[4,128,128]{2,1,0:T(8,128)(2,1)S(1)} collective-permute-done((bf16[4,128,128]{2,1,0:T(8,128)(2,1)S(1)}, bf16[4,128,128]{2,1,0:T(8,128)(2,1)S(1)}, u32[]{:S(2)}, u32[]{:S(2)}) %collective-permute-start) | collective-permute-done | bytes 131104 | tf_op jit(solution)/shard_map/while/body/eval_jaxpr/ppermute | solution.py:10
  296.0 9.7 %collective-permute-done = bf16[4,128,128]{2,1,0:T(8,128)(2,1)S(1)} collective-permute-done((bf16[4,128,128]{2,1,0:T(8,128)(2,1)S(1)}, bf16[4,128,128]{2,1,0:T(8,128)(2,1)S(1)}, u32[]{:S(2)}, u32[]{:S(2)}) %collective-permute-start) | collective-permute-done | bytes 131104 | tf_op jit(solution)/shard_map/while/body/eval_jaxpr/ppermute | solution.py:10
  307.6 3.1 fusion.14
  314.0 9.7 %collective-permute-done = bf16[4,128,128]{2,1,0:T(8,128)(2,1)S(1)} collective-permute-done((bf16[4,128,128]{2,1,0:T(8,128)(2,1)S(1)}, bf16[4,128,128]{2,1,0:T(8,128)(2,1)S(1)}, u32[]{:S(2)}, u32[]{:S(2)}) %collective-permute-start) | collective-permute-done | bytes 131104 | tf_op jit(solution)/shard_map/while/body/eval_jaxpr/ppermute | solution.py:10
  325.7 3.1 fusion.14
  332.1 9.7 %collective-permute-done = bf16[4,128,128]{2,1,0:T(8,128)(2,1)S(1)} collective-permute-done((bf16[4,128,128]{2,1,0:T(8,128)(2,1)S(1)}, bf16[4,128,128]{2,1,0:T(8,128)(2,1)S(1)}, u32[]{:S(2)}, u32[]{:S(2)}) %collective-permute-start) | collective-permute-done | bytes 131104 | tf_op jit(solution)/shard_map/while/body/eval_jaxpr/ppermute | solution.py:10
  343.7 3.1 fusion.14
  350.1 9.7 %collective-permute-done = bf16[4,128,128]{2,1,0:T(8,128)(2,1)S(1)} collective-permute-done((bf16[4,128,128]{2,1,0:T(8,128)(2,1)S(1)}, bf16[4,128,128]{2,1,0:T(8,128)(2,1)S(1)}, u32[]{:S(2)}, u32[]{:S(2)}) %collective-permute-start) | collective-permute-done | bytes 131104 | tf_op jit(solution)/shard_map/while/body/eval_jaxpr/ppermute | solution.py:10
  361.7 3.1 fusion.14
  368.1 9.7 %collective-permute-done = bf16[4,128,128]{2,1,0:T(8,128)(2,1)S(1)} collective-permute-done((bf16[4,128,128]{2,1,0:T(8,128)(2,1)S(1)}, bf16[4,128,128]{2,1,0:T(8,128)(2,1)S(1)}, u32[]{:S(2)}, u32[]{:S(2)}) %collective-permute-start) | collective-permute-done | bytes 131104 | tf_op jit(solution)/shard_map/while/body/eval_jaxpr/ppermute | solution.py:10
  383.0 18.7 %reduce-scatter.2.cloned.1.call-done = f32[3,128,128]{2,1,0:T(8,128)} async-done(((f32[12,128,128]{2,1,0:T(8,128)}), f32[3,128,128]{2,1,0:T(8,128)}) %reduce-scatter.2.cloned.1.call-update) | async-done | bytes 196624 | tf_op jit(solution)/shard_map/reduce_scatter | solution.py:41
  (203 shorter events, 91.5 us)
Async XLA Ops:
  6.5 99.6 %all-gather.3.cloned.1.call-start = ((), (), s32[]{:S(2)}) async-start(), calls=%async_computation.2 | async-start | bytes 1179648 | tf_op jit(solution)/shard_map/all_gather | solution.py:19
  8.1 393.5 %reduce-scatter.2.cloned.1.call-start = ((), (), s32[]{:S(2)}) async-start(), calls=%async_computation.1 | async-start | bytes 983040 | tf_op jit(solution)/shard_map/reduce_scatter | solution.py:41
  109.4 3.1 copy-start
  109.4 3.1 copy-start.1
  112.4 12.9 %collective-permute-start = (bf16[4,128,128]{2,1,0:T(8,128)(2,1)S(1)}, bf16[4,128,128]{2,1,0:T(8,128)(2,1)S(1)}, u32[]{:S(2)}, u32[]{:S(2)}) collective-permute-start(bf16[4,128,128]{2,1,0:T(8,128)(2,1)S(1)} %get-tuple-element.209), channel_id=1, source_target_pairs={{60,0},{0,4},{4,8},{8,12},{12,16},{16,20},{20,24},{24,28},{28,32},... | collective-permute-start | bytes 393224 | tf_op jit(solution)/shard_map/while/body/eval_jaxpr/ppermute | solution.py:10
  130.4 12.9 %collective-permute-start = (bf16[4,128,128]{2,1,0:T(8,128)(2,1)S(1)}, bf16[4,128,128]{2,1,0:T(8,128)(2,1)S(1)}, u32[]{:S(2)}, u32[]{:S(2)}) collective-permute-start(bf16[4,128,128]{2,1,0:T(8,128)(2,1)S(1)} %get-tuple-element.209), channel_id=1, source_target_pairs={{60,0},{0,4},{4,8},{8,12},{12,16},{16,20},{20,24},{24,28},{28,32},... | collective-permute-start | bytes 393224 | tf_op jit(solution)/shard_map/while/body/eval_jaxpr/ppermute | solution.py:10
  148.5 12.9 %collective-permute-start = (bf16[4,128,128]{2,1,0:T(8,128)(2,1)S(1)}, bf16[4,128,128]{2,1,0:T(8,128)(2,1)S(1)}, u32[]{:S(2)}, u32[]{:S(2)}) collective-permute-start(bf16[4,128,128]{2,1,0:T(8,128)(2,1)S(1)} %get-tuple-element.209), channel_id=1, source_target_pairs={{60,0},{0,4},{4,8},{8,12},{12,16},{16,20},{20,24},{24,28},{28,32},... | collective-permute-start | bytes 393224 | tf_op jit(solution)/shard_map/while/body/eval_jaxpr/ppermute | solution.py:10
  166.5 12.9 %collective-permute-start = (bf16[4,128,128]{2,1,0:T(8,128)(2,1)S(1)}, bf16[4,128,128]{2,1,0:T(8,128)(2,1)S(1)}, u32[]{:S(2)}, u32[]{:S(2)}) collective-permute-start(bf16[4,128,128]{2,1,0:T(8,128)(2,1)S(1)} %get-tuple-element.209), channel_id=1, source_target_pairs={{60,0},{0,4},{4,8},{8,12},{12,16},{16,20},{20,24},{24,28},{28,32},... | collective-permute-start | bytes 393224 | tf_op jit(solution)/shard_map/while/body/eval_jaxpr/ppermute | solution.py:10
  184.6 12.9 %collective-permute-start = (bf16[4,128,128]{2,1,0:T(8,128)(2,1)S(1)}, bf16[4,128,128]{2,1,0:T(8,128)(2,1)S(1)}, u32[]{:S(2)}, u32[]{:S(2)}) collective-permute-start(bf16[4,128,128]{2,1,0:T(8,128)(2,1)S(1)} %get-tuple-element.209), channel_id=1, source_target_pairs={{60,0},{0,4},{4,8},{8,12},{12,16},{16,20},{20,24},{24,28},{28,32},... | collective-permute-start | bytes 393224 | tf_op jit(solution)/shard_map/while/body/eval_jaxpr/ppermute | solution.py:10
  202.6 12.9 %collective-permute-start = (bf16[4,128,128]{2,1,0:T(8,128)(2,1)S(1)}, bf16[4,128,128]{2,1,0:T(8,128)(2,1)S(1)}, u32[]{:S(2)}, u32[]{:S(2)}) collective-permute-start(bf16[4,128,128]{2,1,0:T(8,128)(2,1)S(1)} %get-tuple-element.209), channel_id=1, source_target_pairs={{60,0},{0,4},{4,8},{8,12},{12,16},{16,20},{20,24},{24,28},{28,32},... | collective-permute-start | bytes 393224 | tf_op jit(solution)/shard_map/while/body/eval_jaxpr/ppermute | solution.py:10
  220.6 12.9 %collective-permute-start = (bf16[4,128,128]{2,1,0:T(8,128)(2,1)S(1)}, bf16[4,128,128]{2,1,0:T(8,128)(2,1)S(1)}, u32[]{:S(2)}, u32[]{:S(2)}) collective-permute-start(bf16[4,128,128]{2,1,0:T(8,128)(2,1)S(1)} %get-tuple-element.209), channel_id=1, source_target_pairs={{60,0},{0,4},{4,8},{8,12},{12,16},{16,20},{20,24},{24,28},{28,32},... | collective-permute-start | bytes 393224 | tf_op jit(solution)/shard_map/while/body/eval_jaxpr/ppermute | solution.py:10
  238.7 12.9 %collective-permute-start = (bf16[4,128,128]{2,1,0:T(8,128)(2,1)S(1)}, bf16[4,128,128]{2,1,0:T(8,128)(2,1)S(1)}, u32[]{:S(2)}, u32[]{:S(2)}) collective-permute-start(bf16[4,128,128]{2,1,0:T(8,128)(2,1)S(1)} %get-tuple-element.209), channel_id=1, source_target_pairs={{60,0},{0,4},{4,8},{8,12},{12,16},{16,20},{20,24},{24,28},{28,32},... | collective-permute-start | bytes 393224 | tf_op jit(solution)/shard_map/while/body/eval_jaxpr/ppermute | solution.py:10
  256.7 12.9 %collective-permute-start = (bf16[4,128,128]{2,1,0:T(8,128)(2,1)S(1)}, bf16[4,128,128]{2,1,0:T(8,128)(2,1)S(1)}, u32[]{:S(2)}, u32[]{:S(2)}) collective-permute-start(bf16[4,128,128]{2,1,0:T(8,128)(2,1)S(1)} %get-tuple-element.209), channel_id=1, source_target_pairs={{60,0},{0,4},{4,8},{8,12},{12,16},{16,20},{20,24},{24,28},{28,32},... | collective-permute-start | bytes 393224 | tf_op jit(solution)/shard_map/while/body/eval_jaxpr/ppermute | solution.py:10
  274.7 12.9 %collective-permute-start = (bf16[4,128,128]{2,1,0:T(8,128)(2,1)S(1)}, bf16[4,128,128]{2,1,0:T(8,128)(2,1)S(1)}, u32[]{:S(2)}, u32[]{:S(2)}) collective-permute-start(bf16[4,128,128]{2,1,0:T(8,128)(2,1)S(1)} %get-tuple-element.209), channel_id=1, source_target_pairs={{60,0},{0,4},{4,8},{8,12},{12,16},{16,20},{20,24},{24,28},{28,32},... | collective-permute-start | bytes 393224 | tf_op jit(solution)/shard_map/while/body/eval_jaxpr/ppermute | solution.py:10
  292.8 12.9 %collective-permute-start = (bf16[4,128,128]{2,1,0:T(8,128)(2,1)S(1)}, bf16[4,128,128]{2,1,0:T(8,128)(2,1)S(1)}, u32[]{:S(2)}, u32[]{:S(2)}) collective-permute-start(bf16[4,128,128]{2,1,0:T(8,128)(2,1)S(1)} %get-tuple-element.209), channel_id=1, source_target_pairs={{60,0},{0,4},{4,8},{8,12},{12,16},{16,20},{20,24},{24,28},{28,32},... | collective-permute-start | bytes 393224 | tf_op jit(solution)/shard_map/while/body/eval_jaxpr/ppermute | solution.py:10
  310.8 12.9 %collective-permute-start = (bf16[4,128,128]{2,1,0:T(8,128)(2,1)S(1)}, bf16[4,128,128]{2,1,0:T(8,128)(2,1)S(1)}, u32[]{:S(2)}, u32[]{:S(2)}) collective-permute-start(bf16[4,128,128]{2,1,0:T(8,128)(2,1)S(1)} %get-tuple-element.209), channel_id=1, source_target_pairs={{60,0},{0,4},{4,8},{8,12},{12,16},{16,20},{20,24},{24,28},{28,32},... | collective-permute-start | bytes 393224 | tf_op jit(solution)/shard_map/while/body/eval_jaxpr/ppermute | solution.py:10
  328.8 12.9 %collective-permute-start = (bf16[4,128,128]{2,1,0:T(8,128)(2,1)S(1)}, bf16[4,128,128]{2,1,0:T(8,128)(2,1)S(1)}, u32[]{:S(2)}, u32[]{:S(2)}) collective-permute-start(bf16[4,128,128]{2,1,0:T(8,128)(2,1)S(1)} %get-tuple-element.209), channel_id=1, source_target_pairs={{60,0},{0,4},{4,8},{8,12},{12,16},{16,20},{20,24},{24,28},{28,32},... | collective-permute-start | bytes 393224 | tf_op jit(solution)/shard_map/while/body/eval_jaxpr/ppermute | solution.py:10
  346.9 12.9 %collective-permute-start = (bf16[4,128,128]{2,1,0:T(8,128)(2,1)S(1)}, bf16[4,128,128]{2,1,0:T(8,128)(2,1)S(1)}, u32[]{:S(2)}, u32[]{:S(2)}) collective-permute-start(bf16[4,128,128]{2,1,0:T(8,128)(2,1)S(1)} %get-tuple-element.209), channel_id=1, source_target_pairs={{60,0},{0,4},{4,8},{8,12},{12,16},{16,20},{20,24},{24,28},{28,32},... | collective-permute-start | bytes 393224 | tf_op jit(solution)/shard_map/while/body/eval_jaxpr/ppermute | solution.py:10
  364.9 12.9 %collective-permute-start = (bf16[4,128,128]{2,1,0:T(8,128)(2,1)S(1)}, bf16[4,128,128]{2,1,0:T(8,128)(2,1)S(1)}, u32[]{:S(2)}, u32[]{:S(2)}) collective-permute-start(bf16[4,128,128]{2,1,0:T(8,128)(2,1)S(1)} %get-tuple-element.209), channel_id=1, source_target_pairs={{60,0},{0,4},{4,8},{8,12},{12,16},{16,20},{20,24},{24,28},{28,32},... | collective-permute-start | bytes 393224 | tf_op jit(solution)/shard_map/while/body/eval_jaxpr/ppermute | solution.py:10
Sparse Core Ops, SparseCore 0:
  10.6 95.5 all-gather.2
  383.1 18.5 reduce-scatter.1
where the time goes:
time: 412 us; the launch traced here: 409 us
  waiting for transfers between devices  259 us (63%)
  local copies, waits for them, and re-layouts  56 us (14%)
  matrix products  50.3 us (12%)
  starting transfers between devices  28.8 us (7%)
  between operations  13.4 us (3%)
    ppermute x15, waiting for transfers between devices, from_behind(): return lax.ppermute(block, axis, route)  145 us
    all_gather x1, waiting for transfers between devices, body(): right_panel = lax.all_gather(own_tiles, 'row', axis=0, tiled=True)  94.9 us
    dot_general x16, matrix products, contract(): jnp.einsum('moik,mojk->oij', chosen, partner, preferred_element_type=jnp....  50.3 us
    gather x16, local copies, waits for them, and re-layouts, contract(): chosen = jnp.take(left_set, left_index, axis=0)  30.1 us
    ppermute x15, starting transfers between devices, from_behind(): return lax.ppermute(block, axis, route)  28.8 us
    reduce_scatter x1, waiting for transfers between devices, body(): lax.psum_scatter(running, 'depth', scatter_dimension=0, tiled=True)  18.7 us
    gather x16, local copies, waits for them, and re-layouts, contract(): partner = jnp.take(right_panel, right_index, axis=0)  15.9 us
  transfers between devices with their start and end apart: 17, of which 17 were waited for; matrix products, arithmetic and copies ran while one was open for 5% of the time, Pallas kernels for 0%

commit v1 on v0

v1 whole, which is shorter than its diff:
```python
import jax
import jax.numpy as jnp
from jax import lax
from jax.experimental import pallas as pl
from jax.experimental.pallas import tpu as pltpu
from jax.sharding import PartitionSpec as P

MESH = pl.DeviceIdType.MESH
LINE = 8
ROWS = 8
COLS = 16
DEPTH = 4
SLOTS = 4
OUTS = 12
SHIFTS = 16
PAIRS = 4
KEEP = OUTS // DEPTH
CHUNKS = 4
PIECE = SLOTS // CHUNKS
RIGHT = COLS
PASSING = COLS + ROWS
POOL = PASSING + 6
SHIFT_STEP = 8
ORDER = (2, 1, 3, 0)


def arrives(place, step):
    return (step <= place) | (step >= place + 5)


def kernel(
    tiles, pairs, out, pool, partial, landed, load_sem, z_send, z_recv, twin_send, twin_recv,
    y_send, y_recv, x_send, x_recv,
):
    row, col, depth = lax.axis_index("row"), lax.axis_index("col"), lax.axis_index("depth")
    spot, core = col // 2, col % 2
    y, group = row // 2, row % 2

    load = [
        pltpu.make_async_copy(tiles, pool.at[col, 0:SLOTS], load_sem.at[0]),
        pltpu.make_async_copy(tiles, pool.at[RIGHT + row, 0:SLOTS], load_sem.at[1]),
    ]
    for copy in load:
        copy.start()

    def beside(sign):
        edge = spot == (LINE - 1 if sign > 0 else 0)
        return {
            "row": jnp.where(edge, row + 1 - 2 * group, row),
            "col": jnp.where(edge, (0 if sign > 0 else LINE - 1) * 2 + core, col + 2 * sign),
        }

    ways = (beside(1), beside(-1))
    twin = {"col": col + 1 - 2 * core}
    y_peer = [{"row": lax.rem(y + k, 4) * 2 + group} for k in (1, 2, 3)]
    x_peer = [{"depth": lax.rem(depth + k, 4)} for k in (1, 2, 3)]

    barrier = pltpu.get_barrier_semaphore()
    peers = [*ways, twin, *y_peer, *x_peer]
    for peer in peers:
        pl.semaphore_signal(barrier, inc=1, device_id=peer, device_id_type=MESH)

    zero = jnp.zeros((128, 128), jnp.bfloat16)
    for k in range(COLS):
        pool[k, SLOTS] = zero
    pl.semaphore_wait(barrier, len(peers))

    place = (spot, LINE - 1 - spot)
    ahead = [lax.rem(p + 1, LINE) for p in place]
    crossing = [p == LINE - 1 for p in place]

    def slot(way, p, r, step):
        source = lax.rem(p - step + LINE, LINE)
        at = source if way == 0 else LINE - 1 - source
        far = RIGHT + r + 1 - 2 * lax.rem(r, 2) if step == LINE else PASSING + way * 3 + (step - 5)
        if step == 0:
            return col
        if step < 5:
            return at * 2 + core
        return jnp.where(step <= p, at * 2 + core, far)

    def z_copy(way, step, piece):
        theirs = jnp.where(crossing[way], row + 1 - 2 * group, row)
        part = pl.ds(piece * PIECE, PIECE)
        return pltpu.make_async_remote_copy(
            src_ref=pool.at[slot(way, place[way], row, step - 1), part],
            dst_ref=pool.at[slot(way, ahead[way], theirs, step), part],
            send_sem=z_send.at[way, step - 1, piece],
            recv_sem=z_recv.at[way, step - 1, piece],
            device_id=ways[way],
            device_id_type=MESH,
        )

    def z_wait(way, step, piece):
        part = pl.ds(piece * PIECE, PIECE)
        here = pool.at[slot(way, place[way], row, step), part]
        pltpu.make_async_remote_copy(
            src_ref=here, dst_ref=here, send_sem=z_send.at[way, step - 1, piece],
            recv_sem=z_recv.at[way, step - 1, piece], device_id=ways[way], device_id_type=MESH,
        ).wait_recv()

    def twin_copy(at):
        ref = pool.at[at * 2 + core, 0:SLOTS]
        return pltpu.make_async_remote_copy(
            src_ref=ref, dst_ref=ref, send_sem=twin_send.at[at], recv_sem=twin_recv.at[at],
            device_id=twin, device_id_type=MESH,
        )

    def twin_wait(at):
        ref = pool.at[at * 2 + 1 - core, 0:SLOTS]
        pltpu.make_async_remote_copy(
            src_ref=ref, dst_ref=ref, send_sem=twin_send.at[at], recv_sem=twin_recv.at[at],
            device_id=twin, device_id_type=MESH,
        ).wait_recv()

    def y_copy(kind, k):
        ref = pool.at[RIGHT + (row if kind == 0 else row + 1 - 2 * group), 0:SLOTS]
        return pltpu.make_async_remote_copy(
            src_ref=ref, dst_ref=ref, send_sem=y_send.at[kind, k], recv_sem=y_recv.at[kind, k],
            device_id=y_peer[k], device_id_type=MESH,
        )

    def y_wait(kind, k):
        source = lax.rem(y + 3 - k, 4) * 2 + (group if kind == 0 else 1 - group)
        ref = pool.at[RIGHT + source, 0:SLOTS]
        pltpu.make_async_remote_copy(
            src_ref=ref, dst_ref=ref, send_sem=y_send.at[kind, k], recv_sem=y_recv.at[kind, k],
            device_id=y_peer[k], device_id_type=MESH,
        ).wait_recv()

    for copy in load:
        copy.wait()
    for piece in range(CHUNKS):
        for way in range(2):
            @pl.when(arrives(ahead[way], 1))
            def _():
                z_copy(way, 1, piece).start()
    twin_copy(spot).start()
    for k in range(3):
        y_copy(0, k).start()

    for step in range(1, LINE + 1):
        for piece in range(CHUNKS):
            for way in range(2):
                @pl.when(arrives(place[way], step))
                def _():
                    z_wait(way, step, piece)
                    if step < LINE:
                        @pl.when(arrives(ahead[way], step + 1))
                        def _():
                            z_copy(way, step + 1, piece).start()
                    if piece == CHUNKS - 1:
                        if step < LINE:
                            @pl.when(step <= place[way])
                            def _():
                                twin_copy(spot - step if way == 0 else spot + step).start()
                        else:
                            for k in range(3):
                                y_copy(1, k).start()

    for at in range(LINE):
        twin_wait(at)
    for kind in range(2):
        for k in range(3):
            y_wait(kind, k)

    def block(o):
        def some(group_of, total):
            lefts, rights = [], []
            for inner in range(SHIFT_STEP):
                shift = group_of * SHIFT_STEP + inner
                source = lax.rem(col - shift + COLS, COLS)
                for m in range(PAIRS):
                    lefts.append(pool[source, pairs[0, o, m, shift]])
                    pick = pairs[1, o, m, shift]
                    rights.append(pool[RIGHT + pick // SLOTS, lax.rem(pick, SLOTS)])
            return total + lax.dot_general(
                jnp.concatenate(lefts, axis=1), jnp.concatenate(rights, axis=1),
                (((1,), (1,)), ((), ())), preferred_element_type=jnp.float32,
            )

        return lax.fori_loop(0, SHIFTS // SHIFT_STEP, some, jnp.zeros((128, 128), jnp.float32))

    def x_copy(k, i):
        return pltpu.make_async_remote_copy(
            src_ref=partial.at[k - 1, i], dst_ref=landed.at[k - 1, i],
            send_sem=x_send.at[k - 1, i], recv_sem=x_recv.at[k - 1, i],
            device_id=x_peer[k - 1], device_id_type=MESH,
        )

    for k in ORDER:
        owner = lax.rem(depth + k, DEPTH)

        def one(i, _):
            value = block(owner * KEEP + i)
            if k:
                partial[k - 1, i] = value
                x_copy(k, i).start()
            else:
                out[i] = value
            return 0

        lax.fori_loop(0, KEEP, one, 0)

    for k in ORDER[:-1]:
        for i in range(KEEP):
            x_copy(k, i).wait_recv()
    for i in range(KEEP):
        out[i] = out[i] + landed[0, i] + landed[1, i] + landed[2, i]

    for k in ORDER[:-1]:
        for i in range(KEEP):
            x_copy(k, i).wait_send()
    for step in range(1, LINE + 1):
        for way in range(2):
            @pl.when(arrives(ahead[way], step))
            def _():
                for piece in range(CHUNKS):
                    z_copy(way, step, piece).wait_send()
    for at in range(LINE):
        twin_copy(at).wait_send()
    for kind in range(2):
        for k in range(3):
            y_copy(kind, k).wait_send()


def body(a_tiles, pair_lists):
    tiles = a_tiles.reshape(a_tiles.shape[3:])
    pairs = jnp.transpose(pair_lists.reshape(pair_lists.shape[3:]), (1, 3, 2, 0))
    reduced = pl.pallas_call(
        kernel,
        out_shape=jax.ShapeDtypeStruct((KEEP, 128, 128), jnp.float32),
        in_specs=[
            pl.BlockSpec(memory_space=pl.ANY),
            pl.BlockSpec(memory_space=pltpu.SMEM),
        ],
        out_specs=pl.BlockSpec(memory_space=pltpu.VMEM),
        scratch_shapes=[
            pltpu.VMEM((POOL, SLOTS + 1, 128, 128), jnp.bfloat16),
            pltpu.VMEM((DEPTH - 1, KEEP, 128, 128), jnp.float32),
            pltpu.VMEM((DEPTH - 1, KEEP, 128, 128), jnp.float32),
            pltpu.SemaphoreType.DMA((2,)),
            pltpu.SemaphoreType.DMA((2, LINE, CHUNKS)),
            pltpu.SemaphoreType.DMA((2, LINE, CHUNKS)),
            pltpu.SemaphoreType.DMA((LINE,)),
            pltpu.SemaphoreType.DMA((LINE,)),
            pltpu.SemaphoreType.DMA((2, 3)),
            pltpu.SemaphoreType.DMA((2, 3)),
            pltpu.SemaphoreType.DMA((DEPTH - 1, KEEP)),
            pltpu.SemaphoreType.DMA((DEPTH - 1, KEEP)),
        ],
        compiler_params=pltpu.CompilerParams(
            collective_id=0, has_side_effects=True, vmem_limit_bytes=16 << 20
        ),
        name="cannon",
    )(tiles, pairs)
    return reduced.reshape((1, 1) + reduced.shape)


def solution(mesh):
    placed = (
        P("row", "col", "depth", None, None, None),
        P("row", "col", "depth", None, None, None, None),
    )
    return jax.shard_map(
        body,
        mesh=mesh,
        in_specs=placed,
        out_specs=P("row", "col", "depth", None, None),
        check_vma=False,
    )
```

time: 412 us -> 67 us (0.16)
  waiting for transfers between devices: 259 us -> 0 us
  Pallas kernels: 0 us -> 64.4 us
  local copies, waits for them, and re-layouts: 56 us -> 2.38 us
  matrix products: 50.3 us -> 0 us
  starting transfers between devices: 28.8 us -> 0 us
  between operations: 13.4 us -> 0.01 us
    ppermute x15 -> x0, waiting for transfers between devices: 145 us -> none  [from_behind(): return lax.ppermute(block, axis, route)]
    all_gather x1 -> x0, waiting for transfers between devices: 94.9 us -> none  [body(): right_panel = lax.all_gather(own_tiles, 'row', axis=0, tiled=True)]
    pallas_call x0 -> x1, Pallas kernels: none -> 64.4 us  [body(): pl.pallas_call(kernel, out_shape=jax.ShapeDtypeStruct((KEEP, 128, 128), j...]
    dot_general x16 -> x0, matrix products: 50.3 us -> none  [contract(): jnp.einsum('moik,mojk->oij', chosen, partner, preferred_element_type=jnp....]
    gather x32 -> x0, local copies, waits for them, and re-layouts: 46.1 us -> none  [the longest x16 30.1 us: contract(): chosen = jnp.take(left_set, left_index, axis=0)]
    ppermute x15 -> x0, starting transfers between devices: 28.8 us -> none  [from_behind(): return lax.ppermute(block, axis, route)]
    reduce_scatter x1 -> x0, waiting for transfers between devices: 18.7 us -> none  [body(): lax.psum_scatter(running, 'depth', scatter_dimension=0, tiled=True)]
  transfers between devices with their start and end apart: 17 -> 0, of which waited for: 17 -> 0; matrix products, arithmetic and copies ran while one was open for 5% -> 0% of each run, Pallas kernels for 0% -> 0%
where the time goes in v1:
time: 67 us; the launch traced here: 66.8 us
  Pallas kernels  64.4 us (96%)
  local copies, waits for them, and re-layouts  2.38 us (4%)
    pallas_call x1, Pallas kernels, body(): pl.pallas_call(kernel, out_shape=jax.ShapeDtypeStruct((KEEP, 128, 128), j...  64.4 us
    unnamed x5, local copies, waits for them, and re-layouts  2.38 us

profile of v1, /device:TPU:6, one launch (start us, length us, event | category | flops | bytes accessed | tf_op | source)
XLA Modules:
  0.0 66.8 jit_solution(13872031597909803274)
XLA Ops:
  0.0 0.0 copy-start
  0.0 0.9 %copy-done = bf16[1,1,1,4,128,128]{5,4,3,2,1,0:T(8,128)(2,1)S(1)} copy-done((bf16[1,1,1,4,128,128]{5,4,3,2,1,0:T(8,128)(2,1)S(1)}, bf16[1,1,1,4,128,128]{5,4,3,2,1,0:T(8,128)(2,1)}, u32[]{:S(2)}) %copy-start) | copy-done | bytes 131096
  0.9 0.0 copy-start.1
  0.9 0.8 %copy-done.1 = s32[1,1,1,16,2,4,12]{3,5,6,4,2,1,0:T(4,128)S(1)} copy-done((s32[1,1,1,16,2,4,12]{3,5,6,4,2,1,0:T(4,128)S(1)}, s32[1,1,1,16,2,4,12]{3,5,6,4,2,1,0:T(4,128)}, u32[]{:S(2)}) %copy-start.1) | copy-done | bytes 6168
  1.7 64.4 %cannon.1 = f32[3,128,128]{2,1,0:T(8,128)S(1)} custom-call(bf16[4,128,128]{2,1,0:T(8,128)(2,1)S(1)} %bitcast.6, s32[2,12,4,16]{3,2,1,0:T(4,128)S(1)} %bitcast.7), custom_call_target="tpu_custom_call" | custom-call | tf_op jit(solution)/shard_map/cannon/pallas_call | solution.py:230
  66.1 0.7 %copy.4 = f32[1,1,3,128,128]{4,3,2,1,0:T(8,128)} copy(f32[1,1,3,128,128]{4,3,2,1,0:T(8,128)S(1)} %bitcast.5) | data formatting | bytes 393216
Async XLA Ops:
  0.0 0.9 %copy-start = (bf16[1,1,1,4,128,128]{5,4,3,2,1,0:T(8,128)(2,1)S(1)}, bf16[1,1,1,4,128,128]{5,4,3,2,1,0:T(8,128)(2,1)}, u32[]{:S(2)}) copy-start(bf16[1,1,1,4,128,128]{5,4,3,2,1,0:T(8,128)(2,1)} %param.2) | copy-start | bytes 393220
  0.9 0.8 %copy-start.1 = (s32[1,1,1,16,2,4,12]{3,5,6,4,2,1,0:T(4,128)S(1)}, s32[1,1,1,16,2,4,12]{3,5,6,4,2,1,0:T(4,128)}, u32[]{:S(2)}) copy-start(s32[1,1,1,16,2,4,12]{3,5,6,4,2,1,0:T(4,128)} %param.3) | copy-start | bytes 18436

commit v2 on v0

v2 whole, which is shorter than its diff:
```python
import jax
import jax.numpy as jnp
from jax import lax
from jax.experimental import pallas as pl
from jax.experimental.pallas import tpu as pltpu
from jax.sharding import PartitionSpec as P

MESH = pl.DeviceIdType.MESH
LINE = 8
ROWS = 8
COLS = 16
DEPTH = 4
SLOTS = 4
OUTS = 12
SHIFTS = 16
PAIRS = 4
KEEP = OUTS // DEPTH
CHUNKS = 4
PIECE = SLOTS // CHUNKS
RIGHT = COLS
POOL = COLS + ROWS
HALF = LINE // 2
FAR_STEP = 5
SHIFT_STEP = 16
ORDER = (2, 1, 3, 0)


def remote(src, dst, send, recv, device):
    return pltpu.make_async_remote_copy(
        src_ref=src, dst_ref=dst, send_sem=send, recv_sem=recv, device_id=device, device_id_type=MESH
    )


def kernel(
    tiles, pair_table, out, pool, pairs, partial, landed, load_sem, z_send, z_recv, twin_send,
    twin_recv, far_send, far_recv, far_ready, y_send, y_recv, x_send, x_recv,
):
    row, col, depth = lax.axis_index("row"), lax.axis_index("col"), lax.axis_index("depth")
    spot, core = col // 2, col % 2
    y, group = row // 2, row % 2
    other = row + 1 - 2 * group

    load = [
        pltpu.make_async_copy(tiles, pool.at[col, 0:SLOTS], load_sem.at[0]),
        pltpu.make_async_copy(tiles, pool.at[RIGHT + row, 0:SLOTS], load_sem.at[1]),
        pltpu.make_async_copy(pair_table, pairs, load_sem.at[2]),
    ]
    for copy in load:
        copy.start()

    sign = 1 - 2 * core
    place = core * (LINE - 1) + sign * spot
    first, last = place == 0, place == LINE - 1
    after = {"col": col + jnp.where(last, -(LINE - 1), 1) * sign * 2}
    before = {"col": col + jnp.where(first, LINE - 1, -1) * sign * 2}
    twin = {"col": col + sign}
    y_peer = [{"row": lax.rem(y + k, 4) * 2 + group} for k in (1, 2, 3)]
    x_peer = [{"depth": lax.rem(depth + k, 4)} for k in (1, 2, 3)]

    def far_peer(source, plane):
        return {"row": other, "col": (core * (LINE - 1) + sign * source) * 2 + plane}

    relay = {"row": other, "col": jnp.where(spot >= HALF, 1, COLS - 2)}
    partner = {"row": other}
    low = group == 0
    relays = low & last

    barrier = pltpu.get_barrier_semaphore()

    def greet(device):
        pl.semaphore_signal(barrier, inc=1, device_id=device, device_id_type=MESH)

    around = [twin, *y_peer, *x_peer]
    for peer in around:
        greet(peer)

    @pl.when(place > 0)
    def _():
        greet(before)

    @pl.when(low)
    def _():
        greet(partner)

    @pl.when(relays)
    def _():
        for source in range(HALF):
            for plane in range(2):
                greet(far_peer(source, plane))

    pl.semaphore_wait(barrier, len(around) + jnp.where(last, 0, 1) + 2 * group)

    @pl.when(group == 1)
    def _():
        pl.semaphore_signal(far_ready, inc=1, device_id=relay, device_id_type=MESH)

    def at(chip):
        return (core * (LINE - 1) + sign * chip) * 2

    def plane_of(turn):
        return core if turn == 0 else 1 - core

    def z_copy(step, turn, piece):
        ref = pool.at[at(place - step + 1) + plane_of(turn), pl.ds(piece * PIECE, PIECE)]
        return remote(
            ref, ref, z_send.at[step - 1, turn, piece], z_recv.at[step - 1, turn, piece], after
        )

    def z_wait(step, turn, piece):
        here = pool.at[at(place - step) + plane_of(turn), pl.ds(piece * PIECE, PIECE)]
        remote(here, here, z_send.at[step - 1, turn, piece], z_recv.at[step - 1, turn, piece], after).wait_recv()

    def twin_copy(step):
        ref = pool.at[pl.ds((core * (LINE - 1) + sign * (place - step)) * 2, 2), 0:SLOTS]
        return remote(ref, ref, twin_send.at[step], twin_recv.at[step], twin)

    def twin_wait(step):
        ref = pool.at[pl.ds((core * (LINE - 1) + sign * (place + step)) * 2, 2), 0:SLOTS]
        remote(ref, ref, twin_send.at[step], twin_recv.at[step], twin).wait_recv()

    own_copy = remote(
        pool.at[col, 0:SLOTS], pool.at[col, 0:SLOTS], twin_send.at[0], twin_recv.at[0], twin
    )
    twins = pool.at[col + sign, 0:SLOTS]
    own_wait = remote(twins, twins, twin_send.at[0], twin_recv.at[0], twin)

    def far_copy(step, turn, piece):
        part = pl.ds(piece * PIECE, PIECE)
        return remote(
            pool.at[at(place - step) + plane_of(turn), part], pool.at[RIGHT + row, part],
            far_send.at[step - HALF, turn, piece], far_recv.at[piece], far_peer(place - step, plane_of(turn)),
        )

    def direct_copy(piece):
        part = pl.ds(piece * PIECE, PIECE)
        return remote(
            pool.at[col, part], pool.at[RIGHT + row, part], far_send.at[0, 0, piece], far_recv.at[piece], partner
        )

    def pass_far():
        for piece in range(CHUNKS):
            here = pool.at[RIGHT + other, pl.ds(piece * PIECE, PIECE)]
            remote(here, here, far_send.at[0, 0, piece], far_recv.at[piece], partner).wait_recv()
            for k in range(3):
                y_copy(1 + piece, k).start()

    def y_copy(kind, k):
        part = pl.ds((kind - 1) * PIECE, PIECE) if kind else slice(0, SLOTS)
        ref = pool.at[RIGHT + (other if kind else row), part]
        return remote(ref, ref, y_send.at[kind, k], y_recv.at[kind, k], y_peer[k])

    def y_wait(kind, k):
        source = lax.rem(y + 3 - k, 4) * 2 + (1 - group if kind else group)
        part = pl.ds((kind - 1) * PIECE, PIECE) if kind else slice(0, SLOTS)
        ref = pool.at[RIGHT + source, part]
        remote(ref, ref, y_send.at[kind, k], y_recv.at[kind, k], y_peer[k]).wait_recv()

    load[0].wait()
    own_copy.start()

    @pl.when(group == 1)
    def _():
        for piece in range(CHUNKS):
            direct_copy(piece).start()

    @pl.when(place < LINE - 1)
    def _():
        for piece in range(CHUNKS):
            z_copy(1, 0, piece).start()

    load[1].wait()
    for k in range(3):
        y_copy(0, k).start()
    own_wait.wait_recv()

    @pl.when(place < LINE - 1)
    def _():
        for piece in range(CHUNKS):
            z_copy(1, 1, piece).start()

    zero = jnp.zeros((128, 128), jnp.bfloat16)
    for k in range(COLS):
        pool[k, SLOTS] = zero

    for step in range(1, LINE):
        @pl.when(step <= place)
        def _():
            if step == HALF:
                @pl.when(relays)
                def _():
                    pl.semaphore_wait(far_ready, 2 * HALF)

            for turn in range(2):
                for piece in range(CHUNKS):
                    z_wait(step, turn, piece)

                    @pl.when(place < LINE - 1)
                    def _():
                        z_copy(step + 1, turn, piece).start()

                    if step >= HALF:
                        @pl.when(relays)
                        def _():
                            far_copy(step, turn, piece).start()
            twin_copy(step).start()
            if step == FAR_STEP:
                pass_far()

    @pl.when(place < FAR_STEP)
    def _():
        pass_far()

    for step in range(1, LINE):
        @pl.when(place + step < LINE)
        def _():
            twin_wait(step)

    load[2].wait()
    for kind in range(1 + CHUNKS):
        for k in range(3):
            y_wait(kind, k)

    def block(o):
        def some(group_of, total):
            lefts, rights = [], []
            for inner in range(SHIFT_STEP):
                shift = group_of * SHIFT_STEP + inner
                source = lax.rem(col - shift + COLS, COLS)
                for m in range(PAIRS):
                    lefts.append(pool[source, pairs[0, o, m, shift]])
                    pick = pairs[1, o, m, shift]
                    rights.append(pool[RIGHT + pick // SLOTS, lax.rem(pick, SLOTS)])
            value = lax.dot_general(
                jnp.concatenate(lefts, axis=1), jnp.concatenate(rights, axis=1),
                (((1,), (1,)), ((), ())), preferred_element_type=jnp.float32,
            )
            return value if total is None else total + value

        if SHIFT_STEP == SHIFTS:
            return some(0, None)
        return lax.fori_loop(0, SHIFTS // SHIFT_STEP, some, jnp.zeros((128, 128), jnp.float32))

    def x_copy(k, i):
        return remote(
            partial.at[k - 1, i], landed.at[k - 1, i], x_send.at[k - 1, i], x_recv.at[k - 1, i], x_peer[k - 1]
        )

    for k in ORDER:
        owner = lax.rem(depth + k, DEPTH)

        def one(i, _):
            value = block(owner * KEEP + i)
            if k:
                partial[k - 1, i] = value
                x_copy(k, i).start()
            else:
                out[i] = value
            return 0

        lax.fori_loop(0, KEEP, one, 0)

    for k in ORDER[:-1]:
        for i in range(KEEP):
            x_copy(k, i).wait_recv()
    for i in range(KEEP):
        out[i] = out[i] + landed[0, i] + landed[1, i] + landed[2, i]

    for k in ORDER[:-1]:
        for i in range(KEEP):
            x_copy(k, i).wait_send()
    @pl.when(place < LINE - 1)
    def _():
        for step in range(1, LINE):
            @pl.when(step <= place + 1)
            def _():
                for turn in range(2):
                    for piece in range(CHUNKS):
                        z_copy(step, turn, piece).wait_send()

    @pl.when(group == 1)
    def _():
        for piece in range(CHUNKS):
            direct_copy(piece).wait_send()

    @pl.when(relays)
    def _():
        for step in range(HALF, LINE):
            for turn in range(2):
                for piece in range(CHUNKS):
                    far_copy(step, turn, piece).wait_send()

    own_copy.wait_send()
    for step in range(1, LINE):
        @pl.when(step <= place)
        def _():
            twin_copy(step).wait_send()
    for kind in range(1 + CHUNKS):
        for k in range(3):
            y_copy(kind, k).wait_send()


def body(a_tiles, pair_lists):
    tiles = a_tiles.reshape(a_tiles.shape[3:])
    pairs = jnp.transpose(pair_lists.reshape(pair_lists.shape[3:]), (1, 3, 2, 0))
    reduced = pl.pallas_call(
        kernel,
        out_shape=jax.ShapeDtypeStruct((KEEP, 128, 128), jnp.float32),
        in_specs=[
            pl.BlockSpec(memory_space=pltpu.HBM),
            pl.BlockSpec(memory_space=pltpu.HBM),
        ],
        out_specs=pl.BlockSpec(memory_space=pltpu.VMEM),
        scratch_shapes=[
            pltpu.VMEM((POOL, SLOTS + 1, 128, 128), jnp.bfloat16),
            pltpu.SMEM((2, OUTS, PAIRS, SHIFTS), jnp.int32),
            pltpu.VMEM((DEPTH - 1, KEEP, 128, 128), jnp.float32),
            pltpu.VMEM((DEPTH - 1, KEEP, 128, 128), jnp.float32),
            pltpu.SemaphoreType.DMA((3,)),
            pltpu.SemaphoreType.DMA((LINE - 1, 2, CHUNKS)),
            pltpu.SemaphoreType.DMA((LINE - 1, 2, CHUNKS)),
            pltpu.SemaphoreType.DMA((LINE,)),
            pltpu.SemaphoreType.DMA((LINE,)),
            pltpu.SemaphoreType.DMA((LINE - HALF, 2, CHUNKS)),
            pltpu.SemaphoreType.DMA((CHUNKS,)),
            pltpu.SemaphoreType.REGULAR,
            pltpu.SemaphoreType.DMA((1 + CHUNKS, 3)),
            pltpu.SemaphoreType.DMA((1 + CHUNKS, 3)),
            pltpu.SemaphoreType.DMA((DEPTH - 1, KEEP)),
            pltpu.SemaphoreType.DMA((DEPTH - 1, KEEP)),
        ],
        compiler_params=pltpu.CompilerParams(
            collective_id=0, has_side_effects=True, vmem_limit_bytes=60 << 20
        ),
        name="cannon",
    )(tiles, pairs)
    return reduced.reshape((1, 1) + reduced.shape)


def solution(mesh):
    placed = (
        P("row", "col", "depth", None, None, None),
        P("row", "col", "depth", None, None, None, None),
    )
    return jax.shard_map(
        body,
        mesh=mesh,
        in_specs=placed,
        out_specs=P("row", "col", "depth", None, None),
        check_vma=False,
    )
```

time: 412 us -> 56 us (0.14)
  the two profiles are of different devices: /device:TPU:6 before, /device:TPU:481 now
where the time goes in v2:
time: 56 us; the launch traced here: 55.9 us
  Pallas kernels  54.2 us (97%)
  local copies, waits for them, and re-layouts  1.62 us (3%)
    pallas_call x1, Pallas kernels, body(): pl.pallas_call(kernel, out_shape=jax.ShapeDtypeStruct((KEEP, 128, 128), j...  54.2 us
    unnamed x1, local copies, waits for them, and re-layouts  1.62 us

profile of v2, /device:TPU:481, one launch (start us, length us, event | category | flops | bytes accessed | tf_op | source)
XLA Modules:
  0.0 55.9 jit_solution(6322669938376804368)
XLA Ops:
  0.0 54.2 %cannon.1 = f32[3,128,128]{2,1,0:T(8,128)} custom-call(bf16[4,128,128]{2,1,0:T(8,128)(2,1)} %bitcast.6, s32[2,12,4,16]{3,2,1,0:T(4,128)} %bitcast.7), custom_call_target="tpu_custom_call" | custom-call | tf_op jit(solution)/shard_map/cannon/pallas_call | solution.py:305
  54.3 1.6 %copy.4 = f32[1,1,3,128,128]{4,3,2,1,0:T(8,128)} copy(f32[1,1,3,128,128]{4,3,2,1,0:T(8,128)} %bitcast.5) | data formatting | bytes 393216

commit v3 on v2

--- a/solution.py
+++ b/solution.py
@@ -158,11 +158,6 @@
     load[0].wait()
     own_copy.start()
 
-    @pl.when(group == 1)
-    def _():
-        for piece in range(CHUNKS):
-            direct_copy(piece).start()
-
     @pl.when(place < LINE - 1)
     def _():
         for piece in range(CHUNKS):
@@ -177,6 +172,11 @@
     def _():
         for piece in range(CHUNKS):
             z_copy(1, 1, piece).start()
+
+    @pl.when(group == 1)
+    def _():
+        for piece in range(CHUNKS):
+            direct_copy(piece).start()
 
     zero = jnp.zeros((128, 128), jnp.bfloat16)
     for k in range(COLS):

time: 56 us -> 59 us (1.054)
  the two profiles are of different devices: /device:TPU:481 before, /device:TPU:257 now
where the time goes in v3:
time: 59 us; the launch traced here: 58.8 us
  Pallas kernels  57.2 us (97%)
  local copies, waits for them, and re-layouts  1.62 us (3%)
    pallas_call x1, Pallas kernels, body(): pl.pallas_call(kernel, out_shape=jax.ShapeDtypeStruct((KEEP, 128, 128), j...  57.2 us
    unnamed x1, local copies, waits for them, and re-layouts  1.62 us

profile of v3, /device:TPU:257, one launch (start us, length us, event | category | flops | bytes accessed | tf_op | source)
XLA Modules:
  0.0 58.8 jit_solution(871717676772587579)
XLA Ops:
  0.0 57.2 %cannon.1 = f32[3,128,128]{2,1,0:T(8,128)} custom-call(bf16[4,128,128]{2,1,0:T(8,128)(2,1)} %bitcast.6, s32[2,12,4,16]{3,2,1,0:T(4,128)} %bitcast.7), custom_call_target="tpu_custom_call" | custom-call | tf_op jit(solution)/shard_map/cannon/pallas_call | solution.py:305
  57.2 1.6 %copy.4 = f32[1,1,3,128,128]{4,3,2,1,0:T(8,128)} copy(f32[1,1,3,128,128]{4,3,2,1,0:T(8,128)} %bitcast.5) | data formatting | bytes 393216
